TPU v7x, 32 devices: a whole 2x2x4 slice. The times are simulated.
32 devices in a mesh: grp: 2 (over y), mon: 4 (over z), pair: 2 (over x), sub: 2 (over core).
Axes of the slice: x: 2, y: 2, z: 4, core: 2. Of those that a mesh axis runs over, the one named last changes fastest.
Arguments:
- dfactors: bfloat16 [8192, 1024], P('mon', 'sub'), may hold values from -0.5 to 0.5
- block_mask: int32 [64, 1024], P('mon', 'sub'), may hold values 0 or 1
- base_flow: float32 [8192], P('mon'), may hold values from -5 to 5
- branch_row: int32 [1024], replicated, may hold values from 0 to 8191, as said below
- pair_slots: int32 [3072, 2], P(('grp', 'pair')), parts along dimension 0, may hold values from 0 to 1023, as said below
- pair_counts: int32 [4], P(('grp', 'pair')), parts along dimension 0, may hold values from 1 to 768, 1024 in all
Outputs:
- post_flows: bfloat16 [8192, 3072], P(('mon', 'sub'), ('grp', 'pair')), parts along dimension 1
There are 2 independent parts, one for each index of `grp`. A program takes and returns all parts, laid end to end along the dimension named above; an argument that names none is the same for every part. Nothing has to cross between parts.
Inputs may be any that keep to these rules, and one draw needn't show every extreme that they name: `branch_row`: all entries distinct. `pair_slots`: the two candidates of a slot differ; empty slots hold valid pairs too. `pair_counts`: the counts sum to 1024; an owner's live slots are its first ones.
All inputs are finite; a program needn't handle non-finite values. No bound on the sum of `block_mask` or of `pair_counts` on one device may be relied on, other than what follows from the above.
Results may differ from a plain program's by a relative error of at most 0.004.
Values may be sent and summed in bfloat16 or wider, within the bound.
A program may use at most 64 MiB of HBM per device.

v0:
```python
import jax
import jax.numpy as jnp
from jax import lax
from jax.sharding import PartitionSpec as P

BLOCK = 128


def build_shift(col_first, col_count, first_out, second_out, shift_first, shift_second):
    columns = col_first + jnp.arange(col_count, dtype=jnp.int32)[:, None]
    return (
        jnp.where(columns == first_out[None, :], shift_first[None, :], jnp.float32(0.0))
        + jnp.where(columns == second_out[None, :], shift_second[None, :], jnp.float32(0.0))
    ).astype(jnp.bfloat16)


def on_device(dfactors, block_mask, base_flow, branch_row, pair_slots, pair_counts):
    rows_dev, col_width = dfactors.shape
    blocks = block_mask.shape[0]
    masked = (
        dfactors.reshape(blocks, BLOCK, col_width) * block_mask.astype(jnp.bfloat16)[:, None, :]
    ).reshape(rows_dev, col_width)
    row_start = lax.axis_index("mon") * rows_dev
    sub_index = lax.axis_index("sub")
    col_start = sub_index * col_width
    sub_count = lax.axis_size("sub")
    capacity = pair_slots.shape[0]
    own_count = pair_counts[0]
    live_slot = (jnp.arange(capacity, dtype=jnp.int32) < own_count).astype(jnp.float32)
    first_out = pair_slots[:, 0]
    second_out = pair_slots[:, 1]
    first_row = branch_row[first_out]
    second_row = branch_row[second_out]

    def entry(row_ids, col_ids):
        local_row = row_ids - row_start
        local_col = col_ids - col_start
        inside = (
            (local_row >= 0) & (local_row < rows_dev) & (local_col >= 0) & (local_col < col_width)
        )
        value = masked[jnp.clip(local_row, 0, rows_dev - 1), jnp.clip(local_col, 0, col_width - 1)]
        return jnp.where(inside, value.astype(jnp.float32), jnp.float32(0.0))

    def flow_part(row_ids):
        local_row = row_ids - row_start
        inside = (local_row >= 0) & (local_row < rows_dev) & (sub_index == 0)
        return jnp.where(inside, base_flow[jnp.clip(local_row, 0, rows_dev - 1)], jnp.float32(0.0))

    cross_pair = jnp.stack([entry(first_row, second_out), entry(second_row, first_out)], axis=1)
    flow_pair = jnp.stack([flow_part(first_row), flow_part(second_row)], axis=1)
    cross_sum, flow_sum = lax.psum((cross_pair, flow_pair), ("mon", "sub"))
    cross_first = cross_sum[:, 0]
    cross_second = cross_sum[:, 1]
    flow_first = flow_sum[:, 0]
    flow_second = flow_sum[:, 1]
    determinant = 1.0 - cross_first * cross_second
    shift_first = (flow_first + cross_first * flow_second) / determinant
    shift_second = (flow_second + cross_second * flow_first) / determinant
    my_rows = rows_dev // sub_count
    shift = build_shift(col_start, col_width, first_out, second_out, shift_first, shift_second)
    delta = lax.psum_scatter(
        jnp.dot(masked, shift, preferred_element_type=jnp.float32).astype(jnp.bfloat16),
        "sub",
        scatter_dimension=0,
        tiled=True,
    ).astype(jnp.float32)
    flows_half = lax.dynamic_slice_in_dim(base_flow, sub_index * my_rows, my_rows, 0)
    post_flow = flows_half[:, None] + delta
    return (post_flow * live_slot[None, :]).astype(jnp.bfloat16)


def solution(mesh):
    return jax.shard_map(
        on_device,
        mesh=mesh,
        in_specs=(
            P("mon", "sub"),
            P("mon", "sub"),
            P("mon"),
            P(),
            P(("grp", "pair"), None),
            P(("grp", "pair")),
        ),
        out_specs=P(("mon", "sub"), ("grp", "pair")),
        check_vma=False,
    )
```

profile of v0, /device:TPU:0, one launch (start us, length us, event | category | flops | bytes accessed | tf_op | source)
XLA Modules:
  0.0 91.6 jit_solution(11011245030587319538)
XLA Ops:
  6.5 0.0 copy-start
  6.5 0.0 reduce-scatter.2.cloned.1.call-start
  6.5 0.7 fusion.14
  7.3 0.0 copy-done
  7.3 0.0 copy-start.2
  7.3 3.2 %gather_fusion.2 = s32[768]{0:T(1024)S(1)} fusion(s32[1024]{0:T(1024)S(1)} %copy-done, s32[1024]{0:T(1024)S(1)} %pad_clamp_fusion.1), kind=kCustom, calls=%fused_computation.2 | custom fusion | bytes 9216 | tf_op jit(solution)/shard_map/gather | solution.py:33
  10.5 0.0 copy-done.2
  10.5 0.1 slice_reduce_fusion.5
  10.6 0.0 copy-start.3
  10.6 3.2 %gather_fusion = s32[768]{0:T(1024)S(1)} fusion(s32[1024]{0:T(1024)S(1)} %copy-done, s32[1024]{0:T(1024)S(1)} %pad_clamp_fusion.3), kind=kCustom, calls=%fused_computation | custom fusion | bytes 9216 | tf_op jit(solution)/shard_map/gather | solution.py:32
  13.9 0.0 copy-done.3
  13.9 1.7 %bitcast_multiply_fusion = bf16[2048,512]{1,0:T(8,128)(2,1)S(1)} fusion(bf16[2048,512]{1,0:T(8,128)(2,1)} %param.6, bf16[16,512]{1,0:T(8,128)(2,1)S(1)} %convert_element_type.48), kind=kLoop, calls=%fused_computation.8 | loop fusion | flops 1048576 | bytes 4210688 | tf_op jit(solution)/shard_map/mul | solution.py:21
  15.7 0.0 copy-start.1
  15.7 6.7 %gather_fusion.4 = bf16[768]{0:T(1024)(128)(2,1)S(1)} fusion(bf16[2048,512]{1,0:T(8,128)(2,1)S(1)} %bitcast_multiply_fusion, s32[768]{0:T(1024)S(1)} %get-tuple-element.14), kind=kCustom, calls=%fused_computation.4 | custom fusion | bytes 9216 | tf_op jit(solution)/shard_map/gather | solution.py:41
  22.5 6.7 %gather_fusion.5 = bf16[768]{0:T(1024)(128)(2,1)S(1)} fusion(bf16[2048,512]{1,0:T(8,128)(2,1)S(1)} %bitcast_multiply_fusion, s32[768]{0:T(1024)S(1)} %get-tuple-element.6), kind=kCustom, calls=%fused_computation.5 | custom fusion | bytes 9216 | tf_op jit(solution)/shard_map/gather | solution.py:41
  29.2 0.0 copy-done.1
  29.2 4.5 %gather_fusion.1 = f32[768]{0:T(1024)S(1)} fusion(f32[2048]{0:T(1024)S(1)} %copy-done.1, s32[1024]{0:T(1024)S(1)} %pad_clamp_fusion.2), kind=kCustom, calls=%fused_computation.1 | custom fusion | bytes 9216 | tf_op jit(solution)/shard_map/gather | solution.py:47
  33.7 4.5 %gather_fusion.3 = f32[768]{0:T(1024)S(1)} fusion(f32[2048]{0:T(1024)S(1)} %copy-done.1, s32[1024]{0:T(1024)S(1)} %pad_clamp_fusion), kind=kCustom, calls=%fused_computation.3 | custom fusion | bytes 9216 | tf_op jit(solution)/shard_map/gather | solution.py:47
  38.3 30.3 %all-reduce = (f32[768,2]{0,1:T(2,128)S(1)}, f32[768,2]{0,1:T(2,128)S(1)}) all-reduce(f32[768,2]{0,1:T(2,128)S(1)} %pad_maximum_fusion, f32[768,2]{0,1:T(2,128)S(1)} %pad_maximum_fusion.1), channel_id=1, replica_groups=mesh['grp'=2,'mon'=4,'pair'=2,'sub'=2] {'mon','sub'}, use_global_device_ids=true, to_apply=%region_0.1 | all-reduce | flops 3072 | bytes 24576 | tf_op jit(solution)/shard_map/psum | solution.py:51
  68.6 3.6 %convolution_convert_fusion = bf16[2048,768]{1,0:T(8,128)(2,1)} fusion(bf16[2048,512]{1,0:T(8,128)(2,1)S(1)} %bitcast_multiply_fusion, f32[768]{0:T(1024)S(1)} %get-tuple-element.19, s32[768]{0:T(1024)S(1)} %get-tuple-element.8, f32[768]{0:T(1024)S(1)} %get-tuple-element.18, s32[768]{0:T(1024)S(1)} %get-tuple-element.5, s32[512]{0:T(512)S(1)} %iota_add_fusion), kind=kOutput, calls=%fused_computation.6 | convolution fusion | flops 1614544896 | bytes 5257216 | tf_op jit(solution)/shard_map/dot_general | solution.py:62
  72.2 0.0 reduce-scatter.2.cloned.1.call-update
  73.0 8.9 %reduce-scatter.2.cloned.1.call-done = bf16[1024,768]{1,0:T(8,128)(2,1)} async-done(((bf16[2048,768]{1,0:T(8,128)(2,1)}), bf16[1024,768]{1,0:T(8,128)(2,1)}) %reduce-scatter.2.cloned.1.call-update) | async-done | bytes 1572880 | tf_op jit(solution)/shard_map/reduce_scatter | solution.py:61
  81.8 3.0 %multiply_convert_fusion = bf16[1024,768]{1,0:T(8,128)(2,1)} fusion(bf16[1024,768]{1,0:T(8,128)(2,1)} %reduce-scatter.2.cloned.1.call-done, f32[768]{0:T(1024)S(1)} %fusion.12, f32[1024]{0:T(1024)S(1)} %dynamic_slice.3), kind=kLoop, calls=%fused_computation.7 | loop fusion | flops 3145728 | bytes 3152896 | tf_op jit(solution)/shard_map/convert_element_type | solution.py:69
  (20 shorter events, 0.2 us)
Async XLA Ops:
  6.5 0.8 copy-start
  6.5 75.3 %reduce-scatter.2.cloned.1.call-start = ((), (), s32[]{:S(2)}) async-start(), calls=%async_computation.1 | async-start | bytes 4718592 | tf_op jit(solution)/shard_map/reduce_scatter | solution.py:61
  7.3 3.2 %copy-start.2 = (s32[768,2]{0,1:T(2,128)S(1)}, s32[768,2]{0,1:T(2,128)}, u32[]{:S(2)}) copy-start(s32[768,2]{0,1:T(2,128)} %param.10) | copy-start | bytes 18436
  10.6 3.3 %copy-start.3 = (s32[16,512]{1,0:T(8,128)S(1)}, s32[16,512]{1,0:T(8,128)}, u32[]{:S(2)}) copy-start(s32[16,512]{1,0:T(8,128)} %param.7) | copy-start | bytes 98308
  15.7 13.6 %copy-start.1 = (f32[2048]{0:T(1024)S(1)}, f32[2048]{0:T(1024)}, u32[]{:S(2)}) copy-start(f32[2048]{0:T(1024)} %param.8) | copy-start | bytes 24580
Sparse Core Ops, SparseCore 0:
  72.4 9.3 reduce-scatter.1
where the time goes:
time: 91.9 us; the launch traced here: 91.6 us
  blocking collectives  30.3 us (33%)
  local copies, waits for them, and re-layouts  28.9 us (31%)
  between operations  14.3 us (16%)
  waiting for transfers between devices  8.88 us (10%)
  other arithmetic  5.66 us (6%)
  matrix products  3.63 us (4%)
    psum x1, blocking collectives, on_device(): cross_sum, flow_sum = lax.psum((cross_pair, flow_pair), ('mon', 'sub'))  30.3 us
    gather x2, local copies, waits for them, and re-layouts, entry(): masked[jnp.clip(local_row, 0, rows_dev - 1), jnp.clip(local_col, 0, col_w...  13.5 us
    gather x2, local copies, waits for them, and re-layouts, flow_part(): base_flow[jnp.clip(local_row, 0, rows_dev - 1)]  8.93 us
    reduce_scatter x1, waiting for transfers between devices, on_device(): lax.psum_scatter(jnp.dot(masked, shift, preferred_element_type=jnp.float3...  8.86 us
    dot_general x1, matrix products, on_device(): jnp.dot(masked, shift, preferred_element_type=jnp.float32)  3.63 us
    gather x1, local copies, waits for them, and re-layouts, on_device(): second_row = branch_row[second_out]  3.19 us
    gather x1, local copies, waits for them, and re-layouts, on_device(): first_row = branch_row[first_out]  3.19 us
    convert_element_type x1, other arithmetic, on_device(): return (post_flow * live_slot[None, :]).astype(jnp.bfloat16)  2.98 us
  transfers between devices with their start and end apart: 1, of which 1 were waited for; matrix products, arithmetic and copies ran while one was open for 0% of the time, Pallas kernels for 0%

commit v1 on v0

v1 whole, which is shorter than its diff:
```python
import functools

import jax
import jax.numpy as jnp
from jax import lax
from jax.experimental import pallas as pl
from jax.experimental.pallas import tpu as pltpu
from jax.sharding import PartitionSpec as P

BLOCK = 128
MESH = pl.DeviceIdType.MESH
F32 = jnp.float32
BF16 = jnp.bfloat16
I32 = jnp.int32


def lookup(table, index):
    groups = []
    height = table.shape[0]
    for start in range(0, index.shape[1], 128):
        wide = jnp.broadcast_to(index[:, start:start + 128], (height, 128))
        lanes = jnp.take_along_axis(table, wide & 127, axis=1)
        level = lax.broadcasted_iota(I32, (height, 128), 0)
        picked = jnp.where(level == (wide >> 7), lanes, jnp.zeros_like(lanes))
        groups.append(jnp.sum(picked, axis=0, keepdims=True))
    return jnp.concatenate(groups, axis=1)


def kernel(n_mon, n_sub, chunk, df_hbm, mask_hbm, base_hbm, row_hbm, pair_hbm, count_hbm, out_hbm,
           own_df, rest_df, far_df, mask_v, far_mask, base_v, row_v, pair_v, count_s,
           base_wide, product, mask_sum, out_v, flow_own, flow_got, cross_own, cross_got,
           load_sem, part_send, part_recv, flow_send, flow_recv, cross_send, cross_recv, out_sem):
    rows_dev, width = df_hbm.shape
    half = rows_dev // n_sub
    blocks = half // BLOCK
    capacity = pair_hbm.shape[1]
    chunks = capacity // chunk
    n = n_mon * n_sub
    mon = lax.axis_index("mon")
    sub = lax.axis_index("sub")
    me = mon * n_sub + sub
    other = 1 - sub

    def peer(step):
        flat = lax.rem(me + step, n)
        return {"mon": flat // n_sub, "sub": lax.rem(flat, n_sub)}

    barrier = pltpu.get_barrier_semaphore()

    def greet(step, carry):
        pl.semaphore_signal(barrier, inc=1, device_id=peer(step), device_id_type=MESH)
        return carry

    lax.fori_loop(1, n, greet, 0)

    loads = [
        pltpu.make_async_copy(pair_hbm, pair_v, load_sem.at[0]),
        pltpu.make_async_copy(row_hbm, row_v, load_sem.at[1]),
        pltpu.make_async_copy(df_hbm.at[pl.ds(sub * half, half)], own_df, load_sem.at[2]),
        pltpu.make_async_copy(base_hbm.at[pl.ds(sub * blocks, blocks)], base_v, load_sem.at[3]),
        pltpu.make_async_copy(df_hbm.at[pl.ds(other * half, half)], rest_df.at[pl.ds(0, half)], load_sem.at[4]),
        pltpu.make_async_copy(mask_hbm, mask_v, load_sem.at[5]),
        pltpu.make_async_copy(count_hbm, count_s, load_sem.at[6]),
    ]
    for load in loads:
        load.start()
    loads[0].wait()
    loads[1].wait()
    loads[3].wait()
    table = row_v[...]
    base = base_v[...]
    first, second = pair_v[0:1, :], pair_v[1:2, :]
    first_row, second_row = lookup(table, first), lookup(table, second)
    row_start = mon * rows_dev
    flow_start = row_start + sub * half
    flow_own[0:1, :] = lookup(base, first_row - flow_start)
    flow_own[1:2, :] = lookup(base, second_row - flow_start)
    for b in range(blocks):
        base_wide[b * BLOCK:(b + 1) * BLOCK, :] = jnp.broadcast_to(base[b:b + 1, :], (BLOCK, BLOCK)).T

    pl.semaphore_wait(barrier, n - 1)
    partner = {"sub": other}
    part_copies = [
        pltpu.make_async_remote_copy(
            df_hbm.at[pl.ds(other * half, half)], far_df.at[pl.ds(0, half)],
            part_send.at[0], part_recv.at[0], device_id=partner, device_id_type=MESH),
        pltpu.make_async_remote_copy(
            mask_hbm.at[pl.ds(other * blocks, blocks)], far_mask,
            part_send.at[1], part_recv.at[1], device_id=partner, device_id_type=MESH),
    ]
    for copy in part_copies:
        copy.start()

    def send_flow(step, carry):
        pltpu.make_async_remote_copy(
            flow_own, flow_got.at[step - 1], flow_send, flow_recv,
            device_id=peer(step), device_id_type=MESH).start()
        return carry

    lax.fori_loop(1, n, send_flow, 0)

    def send_cross(c):
        def body(step, carry):
            pltpu.make_async_remote_copy(
                cross_own.at[c], cross_got.at[c, step - 1], cross_send.at[c], cross_recv.at[c],
                device_id=peer(step), device_id_type=MESH).start()
            return carry

        lax.fori_loop(1, n, body, 0)

    def both(left, right, c):
        span = slice(c * chunk, (c + 1) * chunk)
        return jnp.concatenate([left[:, span], right[:, span]], axis=1)

    def one_hot(columns, start):
        level = lax.broadcasted_iota(I32, (width, columns.shape[1]), 0) + start
        return jnp.where(level == columns, F32(1), F32(0)).astype(BF16)

    loads[5].wait()
    rest_df[half:, :] = mask_v[...].astype(F32).astype(BF16)
    loads[2].wait()
    loads[4].wait()
    level = lax.broadcasted_iota(I32, (half, 2 * chunk), 0)
    level16 = lax.broadcasted_iota(I32, (n_sub * blocks, 2 * chunk), 0)
    for c in range(chunks):
        columns = both(first, second, c)
        wanted = both(second_row, first_row, c) - row_start
        hot = one_hot(columns, sub * width)
        near = jnp.dot(own_df[...], hot, preferred_element_type=F32)
        product[c] = near.astype(BF16)
        found = jnp.sum(jnp.where(level == wanted - sub * half, near, F32(0)), axis=0, keepdims=True)
        rest = jnp.dot(rest_df[...], hot, preferred_element_type=F32)
        found = found + jnp.sum(
            jnp.where(level == wanted - other * half, rest[:half], F32(0)), axis=0, keepdims=True)
        kept = rest[half:]
        keep = jnp.sum(jnp.where(level16 == (wanted >> 7), kept, F32(0)), axis=0, keepdims=True)
        mask_sum[c] = jnp.where(sub == 0, kept[:blocks], kept[blocks:])
        found = found * keep
        cross_own[c, 0:1, :] = found[:, chunk:]
        cross_own[c, 1:2, :] = found[:, :chunk]
        send_cross(c)

    for copy in part_copies:
        copy.wait_recv()
    far_df[half:half + blocks, :] = far_mask[...].astype(F32).astype(BF16)
    for c in range(chunks):
        hot = one_hot(both(first, second, c), other * width)
        far = jnp.dot(far_df[...], hot, preferred_element_type=F32)
        product[c] = (product[c].astype(F32) + far[:half]).astype(BF16)
        mask_sum[c] = mask_sum[c] + far[half:half + blocks]

    pltpu.make_async_copy(flow_got, flow_got, flow_recv).wait()
    loads[6].wait()
    flow = flow_own[...] + jnp.sum(flow_got[...], axis=0)
    live = (lax.broadcasted_iota(I32, (1, capacity), 1) < count_s[0]).astype(F32)
    outs = []
    for c in range(chunks):
        span = slice(c * chunk, (c + 1) * chunk)
        pltpu.make_async_copy(cross_got.at[c], cross_got.at[c], cross_recv.at[c]).wait()
        cross = cross_own[c] + jnp.sum(cross_got[c], axis=0)
        cross_first, cross_second = cross[0:1], cross[1:2]
        flow_first, flow_second = flow[0:1, span], flow[1:2, span]
        determinant = 1.0 - cross_first * cross_second
        shift_first = (flow_first + cross_first * flow_second) / determinant
        shift_second = (flow_second + cross_second * flow_first) / determinant
        alive = live[:, span]
        shift_first = shift_first.astype(BF16).astype(F32) * alive
        shift_second = shift_second.astype(BF16).astype(F32) * alive
        keep = mask_sum[c]
        for b in range(blocks):
            rows = slice(b * BLOCK, (b + 1) * BLOCK)
            flows = jnp.concatenate([base_wide[rows, :]] * (chunk // BLOCK), axis=1)
            e1 = shift_first * keep[b:b + 1, :chunk]
            e2 = shift_second * keep[b:b + 1, chunk:]
            value = flows * alive + product[c, rows, :chunk].astype(F32) * e1
            value = value + product[c, rows, chunk:].astype(F32) * e2
            out_v[rows, span] = value.astype(BF16)
        outs.append(pltpu.make_async_copy(out_v.at[:, span], out_hbm.at[:, span], out_sem.at[c]))
        outs[-1].start()

    for copy in part_copies:
        copy.wait_send()
    pltpu.make_async_copy(flow_got, flow_got, flow_send).wait()
    for c in range(chunks):
        pltpu.make_async_copy(cross_got.at[c], cross_got.at[c], cross_send.at[c]).wait()
    for copy in outs:
        copy.wait()


def on_device(n_mon, n_sub, dfactors, block_mask, base_flow, branch_row, pair_slots, pair_counts):
    rows_dev, width = dfactors.shape
    half = rows_dev // n_sub
    blocks = half // BLOCK
    capacity = pair_slots.shape[0]
    chunk = 256 if capacity % 256 == 0 else BLOCK
    chunks = capacity // chunk
    n = n_mon * n_sub
    any_spec = pl.BlockSpec(memory_space=pltpu.HBM)
    dma = pltpu.SemaphoreType.DMA
    return pl.pallas_call(
        functools.partial(kernel, n_mon, n_sub, chunk),
        out_shape=jax.ShapeDtypeStruct((half, capacity), BF16),
        in_specs=[any_spec] * 6,
        out_specs=any_spec,
        scratch_shapes=[
            pltpu.VMEM((half, width), BF16),
            pltpu.VMEM((half + n_sub * blocks, width), BF16),
            pltpu.VMEM((half + n_sub * blocks, width), BF16),
            pltpu.VMEM((n_sub * blocks, width), I32),
            pltpu.VMEM((blocks, width), I32),
            pltpu.VMEM((blocks, BLOCK), F32),
            pltpu.VMEM((branch_row.shape[0] // BLOCK, BLOCK), I32),
            pltpu.VMEM((2, capacity), I32),
            pltpu.SMEM((1,), I32),
            pltpu.VMEM((half, BLOCK), F32),
            pltpu.VMEM((chunks, half, 2 * chunk), BF16),
            pltpu.VMEM((chunks, blocks, 2 * chunk), F32),
            pltpu.VMEM((half, capacity), BF16),
            pltpu.VMEM((2, capacity), F32),
            pltpu.VMEM((n - 1, 2, capacity), F32),
            pltpu.VMEM((chunks, 2, chunk), F32),
            pltpu.VMEM((chunks, n - 1, 2, chunk), F32),
            dma((7,)), dma((2,)), dma((2,)), dma, dma, dma((chunks,)), dma((chunks,)), dma((chunks,)),
        ],
        compiler_params=pltpu.CompilerParams(
            collective_id=0, has_side_effects=True, vmem_limit_bytes=60 * 1024 * 1024),
    )(dfactors, block_mask, base_flow.reshape(-1, BLOCK), branch_row.reshape(-1, BLOCK),
      pair_slots.T, pair_counts)


def solution(mesh):
    return jax.shard_map(
        functools.partial(on_device, mesh.shape["mon"], mesh.shape["sub"]),
        mesh=mesh,
        in_specs=(
            P("mon", "sub"),
            P("mon", "sub"),
            P("mon"),
            P(),
            P(("grp", "pair"), None),
            P(("grp", "pair")),
        ),
        out_specs=P(("mon", "sub"), ("grp", "pair")),
        check_vma=False,
    )
```

time: 91.9 us -> 17.7 us (0.19)
  blocking collectives: 30.3 us -> 0 us
  local copies, waits for them, and re-layouts: 28.9 us -> 2.65 us
  Pallas kernels: 0 us -> 14.2 us
  between operations: 14.3 us -> 0.66 us
  waiting for transfers between devices: 8.88 us -> 0 us
  other arithmetic: 5.66 us -> 0 us
  matrix products: 3.63 us -> 0 us
    psum x1 -> x0, blocking collectives: 30.3 us -> none  [on_device(): cross_sum, flow_sum = lax.psum((cross_pair, flow_pair), ('mon', 'sub'))]
    gather x6 -> x0, local copies, waits for them, and re-layouts: 28.8 us -> none  [the longest x2 13.5 us: entry(): masked[jnp.clip(local_row, 0, rows_dev - 1), jnp.clip(local_col, 0, col_w...]
    pallas_call x0 -> x1, Pallas kernels: none -> 14.2 us  [on_device(): pl.pallas_call(functools.partial(kernel, n_mon, n_sub, chunk), out_shape=...]
    reduce_scatter x1 -> x0, waiting for transfers between devices: 8.86 us -> none  [on_device(): lax.psum_scatter(jnp.dot(masked, shift, preferred_element_type=jnp.float3...]
    dot_general x1 -> x0, matrix products: 3.63 us -> none  [on_device(): jnp.dot(masked, shift, preferred_element_type=jnp.float32)]
    convert_element_type x5 -> x0, other arithmetic: 2.99 us -> none  [the longest x1 2.98 us: on_device(): return (post_flow * live_slot[None, :]).astype(jnp.bfloat16)]
    unnamed x8 -> x1, local copies, waits for them, and re-layouts: 0.02 us -> 2.65 us
    mul x1 -> x0, other arithmetic: 1.74 us -> none  [on_device(): dfactors.reshape(blocks, BLOCK, col_width)]
  transfers between devices with their start and end apart: 1 -> 0, of which waited for: 1 -> 0; matrix products, arithmetic and copies ran while one was open for 0% -> 0% of each run, Pallas kernels for 0% -> 0%
where the time goes in v1:
time: 17.7 us; the launch traced here: 17.5 us
  Pallas kernels  14.2 us (80%)
  local copies, waits for them, and re-layouts  2.65 us (15%)
  between operations  0.66 us (4%)
    pallas_call x1, Pallas kernels, on_device(): pl.pallas_call(functools.partial(kernel, n_mon, n_sub, chunk), out_shape=...  14.2 us
    unnamed x1, local copies, waits for them, and re-layouts  2.65 us

profile of v1, /device:TPU:0, one launch (start us, length us, event | category | flops | bytes accessed | tf_op | source)
XLA Modules:
  0.0 17.5 jit_solution(18065076997865412066)
XLA Ops:
  0.7 14.2 %shard_map.64 = bf16[1024,768]{1,0:T(8,128)(2,1)} custom-call(bf16[2048,512]{1,0:T(8,128)(2,1)} %df_hbm.1, s32[16,512]{1,0:T(8,128)} %mask_hbm.1, f32[16,128]{1,0:T(8,128)} %bitcast.3, s32[8,128]{1,0:T(8,128)} %bitcast.5, s32[2,768]{1,0:T(2,128)} %bitcast.4, s32[1]{0:T(128)S(6)} %copy.8.count_hbm), custom_call_target="tpu_custom_call" | custom-call | tf_op jit(solution)/shard_map/pallas_call | solution.py:200
  14.8 2.7 %copy.9 = bf16[1024,768]{1,0:T(8,128)(2,1)} copy(bf16[1024,768]{1,0:T(8,128)(2,1)} %shard_map.64) | data formatting | bytes 3145728

commit v2 on v1

--- a/solution.py
+++ b/solution.py
@@ -26,10 +26,10 @@
     return jnp.concatenate(groups, axis=1)
 
 
-def kernel(n_mon, n_sub, chunk, df_hbm, mask_hbm, base_hbm, row_hbm, pair_hbm, count_hbm, out_hbm,
+def kernel(n_mon, n_sub, chunk, df_hbm, mask_hbm, base_hbm, row_hbm, pair_hbm, count_hbm, out_v,
            own_df, rest_df, far_df, mask_v, far_mask, base_v, row_v, pair_v, count_s,
-           base_wide, product, mask_sum, out_v, flow_own, flow_got, cross_own, cross_got,
-           load_sem, part_send, part_recv, flow_send, flow_recv, cross_send, cross_recv, out_sem):
+           base_wide, product, mask_sum, flow_own, flow_got, cross_own, cross_got,
+           load_sem, part_send, part_recv, flow_send, flow_recv, cross_send, cross_recv):
     rows_dev, width = df_hbm.shape
     half = rows_dev // n_sub
     blocks = half // BLOCK
@@ -153,7 +153,6 @@
     loads[6].wait()
     flow = flow_own[...] + jnp.sum(flow_got[...], axis=0)
     live = (lax.broadcasted_iota(I32, (1, capacity), 1) < count_s[0]).astype(F32)
-    outs = []
     for c in range(chunks):
         span = slice(c * chunk, (c + 1) * chunk)
         pltpu.make_async_copy(cross_got.at[c], cross_got.at[c], cross_recv.at[c]).wait()
@@ -175,16 +174,12 @@
             value = flows * alive + product[c, rows, :chunk].astype(F32) * e1
             value = value + product[c, rows, chunk:].astype(F32) * e2
             out_v[rows, span] = value.astype(BF16)
-        outs.append(pltpu.make_async_copy(out_v.at[:, span], out_hbm.at[:, span], out_sem.at[c]))
-        outs[-1].start()
 
     for copy in part_copies:
         copy.wait_send()
     pltpu.make_async_copy(flow_got, flow_got, flow_send).wait()
     for c in range(chunks):
         pltpu.make_async_copy(cross_got.at[c], cross_got.at[c], cross_send.at[c]).wait()
-    for copy in outs:
-        copy.wait()
 
 
 def on_device(n_mon, n_sub, dfactors, block_mask, base_flow, branch_row, pair_slots, pair_counts):
@@ -197,11 +192,11 @@
     n = n_mon * n_sub
     any_spec = pl.BlockSpec(memory_space=pltpu.HBM)
     dma = pltpu.SemaphoreType.DMA
-    return pl.pallas_call(
+    made = pl.pallas_call(
         functools.partial(kernel, n_mon, n_sub, chunk),
-        out_shape=jax.ShapeDtypeStruct((half, capacity), BF16),
+        out_shape=pltpu.VMEM((half, capacity), BF16),
         in_specs=[any_spec] * 6,
-        out_specs=any_spec,
+        out_specs=pl.BlockSpec(memory_space=pltpu.VMEM),
         scratch_shapes=[
             pltpu.VMEM((half, width), BF16),
             pltpu.VMEM((half + n_sub * blocks, width), BF16),
@@ -215,17 +210,17 @@
             pltpu.VMEM((half, BLOCK), F32),
             pltpu.VMEM((chunks, half, 2 * chunk), BF16),
             pltpu.VMEM((chunks, blocks, 2 * chunk), F32),
-            pltpu.VMEM((half, capacity), BF16),
             pltpu.VMEM((2, capacity), F32),
             pltpu.VMEM((n - 1, 2, capacity), F32),
             pltpu.VMEM((chunks, 2, chunk), F32),
             pltpu.VMEM((chunks, n - 1, 2, chunk), F32),
-            dma((7,)), dma((2,)), dma((2,)), dma, dma, dma((chunks,)), dma((chunks,)), dma((chunks,)),
+            dma((7,)), dma((2,)), dma((2,)), dma, dma, dma((chunks,)), dma((chunks,)),
         ],
         compiler_params=pltpu.CompilerParams(
             collective_id=0, has_side_effects=True, vmem_limit_bytes=60 * 1024 * 1024),
     )(dfactors, block_mask, base_flow.reshape(-1, BLOCK), branch_row.reshape(-1, BLOCK),
       pair_slots.T, pair_counts)
+    return made
 
 
 def solution(mesh):

time: 17.7 us -> 15.3 us (0.86)
  local copies, waits for them, and re-layouts: 2.65 us -> 1.15 us
  Pallas kernels: 14.2 us -> 13.3 us
    unnamed x1, local copies, waits for them, and re-layouts: 2.65 us -> 1.15 us
    pallas_call x1, Pallas kernels: 14.2 us -> 13.3 us  [on_device(): pl.pallas_call(functools.partial(kernel, n_mon, n_sub, chunk), out_shape=...]
where the time goes in v2:
time: 15.3 us; the launch traced here: 15.1 us
  Pallas kernels  13.3 us (87%)
  local copies, waits for them, and re-layouts  1.15 us (8%)
  between operations  0.66 us (4%)
    pallas_call x1, Pallas kernels, on_device(): pl.pallas_call(functools.partial(kernel, n_mon, n_sub, chunk), out_shape=...  13.3 us
    unnamed x1, local copies, waits for them, and re-layouts  1.15 us

profile of v2, /device:TPU:0, one launch (start us, length us, event | category | flops | bytes accessed | tf_op | source)
XLA Modules:
  0.0 15.1 jit_solution(17727275927588694519)
XLA Ops:
  0.7 13.3 %shard_map.64 = bf16[1024,768]{1,0:T(8,128)(2,1)S(1)} custom-call(bf16[2048,512]{1,0:T(8,128)(2,1)} %df_hbm.1, s32[16,512]{1,0:T(8,128)} %mask_hbm.1, f32[16,128]{1,0:T(8,128)} %bitcast.3, s32[8,128]{1,0:T(8,128)} %bitcast.5, s32[2,768]{1,0:T(2,128)} %bitcast.4, s32[1]{0:T(128)S(6)} %copy.9.count_hbm), custom_call_target="tpu_custom_call" | custom-call | tf_op jit(solution)/shard_map/pallas_call | solution.py:195
  13.9 1.1 %copy.8 = bf16[1024,768]{1,0:T(8,128)(2,1)} copy(bf16[1024,768]{1,0:T(8,128)(2,1)S(1)} %shard_map.64) | data formatting | bytes 3145728

commit v3 on v2

--- a/solution.py
+++ b/solution.py
@@ -26,9 +26,43 @@
     return jnp.concatenate(groups, axis=1)
 
 
-def kernel(n_mon, n_sub, chunk, df_hbm, mask_hbm, base_hbm, row_hbm, pair_hbm, count_hbm, out_v,
+def flows_of(b, base_wide, product, effect, alive):
+    rows = slice(b * BLOCK, (b + 1) * BLOCK)
+    chunk = product.shape[1] // 2
+    flows = jnp.concatenate([base_wide[rows, :]] * (chunk // BLOCK), axis=1)
+    value = flows * alive + product[rows, :chunk].astype(F32) * effect[b:b + 1, :chunk]
+    value = value + product[rows, chunk:].astype(F32) * effect[b:b + 1, chunk:]
+    return value.astype(BF16)
+
+
+def last_kernel(pieces, ready, product, effect, base_wide, alive, out_hbm, last, sems):
+    chunks, half, pair_width = product.shape
+    chunk = pair_width // 2
+    split = (chunks - 1) * chunk
+    rows = half // pieces
+    copies = []
+    if chunks > 1:
+        for piece in range(2):
+            span = pl.ds(piece * (half // 2), half // 2)
+            columns = pl.ds(0, split)
+            copies.append(pltpu.make_async_copy(
+                ready.at[span, columns], out_hbm.at[span, columns], sems.at[pieces + piece]))
+            copies[-1].start()
+    for piece in range(pieces):
+        for b in range(piece * rows // BLOCK, (piece + 1) * rows // BLOCK):
+            last[b * BLOCK:(b + 1) * BLOCK, :] = flows_of(
+                b, base_wide, product.at[chunks - 1], effect, alive[...])
+        span = pl.ds(piece * rows, rows)
+        copies.append(pltpu.make_async_copy(
+            last.at[span], out_hbm.at[span, pl.ds(split, chunk)], sems.at[piece]))
+        copies[-1].start()
+    for copy in copies:
+        copy.wait()
+
+
+def kernel(n_mon, n_sub, chunk, df_hbm, mask_hbm, base_hbm, row_hbm, pair_hbm, count_hbm, out_v, product, effect, base_wide, alive_v,
            own_df, rest_df, far_df, mask_v, far_mask, base_v, row_v, pair_v, count_s,
-           base_wide, product, mask_sum, flow_own, flow_got, cross_own, cross_got,
+           mask_sum, flow_own, flow_got, cross_own, cross_got,
            load_sem, part_send, part_recv, flow_send, flow_recv, cross_send, cross_recv):
     rows_dev, width = df_hbm.shape
     half = rows_dev // n_sub
@@ -75,10 +109,7 @@
     flow_start = row_start + sub * half
     flow_own[0:1, :] = lookup(base, first_row - flow_start)
     flow_own[1:2, :] = lookup(base, second_row - flow_start)
-    for b in range(blocks):
-        base_wide[b * BLOCK:(b + 1) * BLOCK, :] = jnp.broadcast_to(base[b:b + 1, :], (BLOCK, BLOCK)).T
-
-    pl.semaphore_wait(barrier, n - 1)
+
     partner = {"sub": other}
     part_copies = [
         pltpu.make_async_remote_copy(
@@ -88,15 +119,15 @@
             mask_hbm.at[pl.ds(other * blocks, blocks)], far_mask,
             part_send.at[1], part_recv.at[1], device_id=partner, device_id_type=MESH),
     ]
-    for copy in part_copies:
-        copy.start()
-
     def send_flow(step, carry):
         pltpu.make_async_remote_copy(
             flow_own, flow_got.at[step - 1], flow_send, flow_recv,
             device_id=peer(step), device_id_type=MESH).start()
         return carry
 
+    pl.semaphore_wait(barrier, n - 1)
+    for copy in part_copies:
+        copy.start()
     lax.fori_loop(1, n, send_flow, 0)
 
     def send_cross(c):
@@ -119,7 +150,6 @@
     loads[5].wait()
     rest_df[half:, :] = mask_v[...].astype(F32).astype(BF16)
     loads[2].wait()
-    loads[4].wait()
     level = lax.broadcasted_iota(I32, (half, 2 * chunk), 0)
     level16 = lax.broadcasted_iota(I32, (n_sub * blocks, 2 * chunk), 0)
     for c in range(chunks):
@@ -129,6 +159,8 @@
         near = jnp.dot(own_df[...], hot, preferred_element_type=F32)
         product[c] = near.astype(BF16)
         found = jnp.sum(jnp.where(level == wanted - sub * half, near, F32(0)), axis=0, keepdims=True)
+        if c == 0:
+            loads[4].wait()
         rest = jnp.dot(rest_df[...], hot, preferred_element_type=F32)
         found = found + jnp.sum(
             jnp.where(level == wanted - other * half, rest[:half], F32(0)), axis=0, keepdims=True)
@@ -139,6 +171,8 @@
         cross_own[c, 0:1, :] = found[:, chunk:]
         cross_own[c, 1:2, :] = found[:, :chunk]
         send_cross(c)
+    for b in range(blocks):
+        base_wide[b * BLOCK:(b + 1) * BLOCK, :] = jnp.broadcast_to(base[b:b + 1, :], (BLOCK, BLOCK)).T
 
     for copy in part_copies:
         copy.wait_recv()
@@ -166,14 +200,14 @@
         shift_first = shift_first.astype(BF16).astype(F32) * alive
         shift_second = shift_second.astype(BF16).astype(F32) * alive
         keep = mask_sum[c]
-        for b in range(blocks):
-            rows = slice(b * BLOCK, (b + 1) * BLOCK)
-            flows = jnp.concatenate([base_wide[rows, :]] * (chunk // BLOCK), axis=1)
-            e1 = shift_first * keep[b:b + 1, :chunk]
-            e2 = shift_second * keep[b:b + 1, chunk:]
-            value = flows * alive + product[c, rows, :chunk].astype(F32) * e1
-            value = value + product[c, rows, chunk:].astype(F32) * e2
-            out_v[rows, span] = value.astype(BF16)
+        effect[:, :chunk] = shift_first * keep[:, :chunk]
+        effect[:, chunk:] = shift_second * keep[:, chunk:]
+        if c == chunks - 1:
+            alive_v[...] = alive
+        else:
+            for b in range(blocks):
+                rows = slice(b * BLOCK, (b + 1) * BLOCK)
+                out_v[rows, span] = flows_of(b, base_wide, product.at[c], effect, alive)
 
     for copy in part_copies:
         copy.wait_send()
@@ -191,12 +225,19 @@
     chunks = capacity // chunk
     n = n_mon * n_sub
     any_spec = pl.BlockSpec(memory_space=pltpu.HBM)
+    vmem_spec = pl.BlockSpec(memory_space=pltpu.VMEM)
     dma = pltpu.SemaphoreType.DMA
     made = pl.pallas_call(
         functools.partial(kernel, n_mon, n_sub, chunk),
-        out_shape=pltpu.VMEM((half, capacity), BF16),
+        out_shape=[
+            pltpu.VMEM((half, capacity), BF16),
+            pltpu.VMEM((chunks, half, 2 * chunk), BF16),
+            pltpu.VMEM((blocks, 2 * chunk), F32),
+            pltpu.VMEM((half, BLOCK), F32),
+            pltpu.VMEM((1, chunk), F32),
+        ],
         in_specs=[any_spec] * 6,
-        out_specs=pl.BlockSpec(memory_space=pltpu.VMEM),
+        out_specs=[vmem_spec] * 5,
         scratch_shapes=[
             pltpu.VMEM((half, width), BF16),
             pltpu.VMEM((half + n_sub * blocks, width), BF16),
@@ -207,8 +248,6 @@
             pltpu.VMEM((branch_row.shape[0] // BLOCK, BLOCK), I32),
             pltpu.VMEM((2, capacity), I32),
             pltpu.SMEM((1,), I32),
-            pltpu.VMEM((half, BLOCK), F32),
-            pltpu.VMEM((chunks, half, 2 * chunk), BF16),
             pltpu.VMEM((chunks, blocks, 2 * chunk), F32),
             pltpu.VMEM((2, capacity), F32),
             pltpu.VMEM((n - 1, 2, capacity), F32),
@@ -217,10 +256,18 @@
             dma((7,)), dma((2,)), dma((2,)), dma, dma, dma((chunks,)), dma((chunks,)),
         ],
         compiler_params=pltpu.CompilerParams(
-            collective_id=0, has_side_effects=True, vmem_limit_bytes=60 * 1024 * 1024),
+            collective_id=0, has_side_effects=True, vmem_limit_bytes=int(58.8 * 1024 * 1024)),
     )(dfactors, block_mask, base_flow.reshape(-1, BLOCK), branch_row.reshape(-1, BLOCK),
       pair_slots.T, pair_counts)
-    return made
+    pieces = 2
+    return pl.pallas_call(
+        functools.partial(last_kernel, pieces),
+        out_shape=jax.ShapeDtypeStruct((half, capacity), BF16),
+        in_specs=[vmem_spec] * 5,
+        out_specs=any_spec,
+        scratch_shapes=[pltpu.VMEM((half, chunk), BF16), dma((pieces + 2,))],
+        compiler_params=pltpu.CompilerParams(vmem_limit_bytes=8 * 1024 * 1024),
+    )(*[pltpu.with_memory_space_constraint(array, pltpu.VMEM) for array in made])
 
 
 def solution(mesh):

time: 15.3 us -> 15 us (0.980)
  local copies, waits for them, and re-layouts: 1.15 us -> 0 us
  Pallas kernels: 13.3 us -> 14.2 us
    pallas_call x0 -> x1, Pallas kernels: none -> 1.17 us  [on_device(): pl.pallas_call(functools.partial(last_kernel, pieces), out_shape=jax.Shap...]
    unnamed x1 -> x0, local copies, waits for them, and re-layouts: 1.15 us -> none
    pallas_call x1, Pallas kernels: 13.3 us -> 13 us  [on_device(): pl.pallas_call(functools.partial(kernel, n_mon, n_sub, chunk), out_shape=...]
where the time goes in v3:
time: 15 us; the launch traced here: 14.8 us
  Pallas kernels  14.2 us (95%)
  between operations  0.66 us (4%)
    pallas_call x1, Pallas kernels, on_device(): pl.pallas_call(functools.partial(kernel, n_mon, n_sub, chunk), out_shape=...  13 us
    pallas_call x1, Pallas kernels, on_device(): pl.pallas_call(functools.partial(last_kernel, pieces), out_shape=jax.Shap...  1.17 us

profile of v3, /device:TPU:0, one launch (start us, length us, event | category | flops | bytes accessed | tf_op | source)
XLA Modules:
  0.0 14.8 jit_solution(15853138429974699895)
XLA Ops:
  0.7 13.0 %shard_map.64 = (bf16[1024,768]{1,0:T(8,128)(2,1)S(1)}, bf16[3,1024,512]{2,1,0:T(8,128)(2,1)S(1)}, f32[8,512]{1,0:T(8,128)S(1)}, f32[1024,128]{1,0:T(8,128)S(1)}, f32[1,256]{1,0:T(1,128)S(1)}) custom-call(bf16[2048,512]{1,0:T(8,128)(2,1)} %df_hbm.1, s32[16,512]{1,0:T(8,128)} %mask_hbm.1, f32[16,128]{1,0:T(8,128)} %bitcast.3, s32[8,128]{1,0:T(8,128)} %bitcast.5, ...), custom_call_target="tpu_custom_call" | custom-call | tf_op jit(solution)/shard_map/pallas_call | solution.py:230
  13.7 1.2 %shard_map.65 = bf16[1024,768]{1,0:T(8,128)(2,1)} custom-call(bf16[1024,768]{1,0:T(8,128)(2,1)S(1)} %get-tuple-element.10.ready, bf16[3,1024,512]{2,1,0:T(8,128)(2,1)S(1)} %get-tuple-element.11.product, f32[8,512]{1,0:T(8,128)S(1)} %get-tuple-element.12.effect, f32[1024,128]{1,0:T(8,128)S(1)} %get-tuple-element.13.base_wide, ...), custom_call_target="tpu_custom_call" | custom-call | tf_op jit(solution)/shard_map/pallas_call | solution.py:263
